TPU v7x, 256 devices: a whole 4x4x8 slice. The times are simulated.
256 devices in a mesh: leaf: 64 (over x, z, core), front: 4 (over y).
Axes of the slice: x: 4, y: 4, z: 8, core: 2. Of those that a mesh axis runs over, the one named last changes fastest.
Arguments:
- leaf_update: float32 [65536, 1024], P('leaf'), as said below
- separator_rows_1: float32 [16384, 1536], P(('leaf', 'front')), as said below
- remaining_rows_1: float32 [32768, 1536], P(('leaf', 'front'))
- separator_rows_2: float32 [8192, 1536], P(('leaf', 'front')), as said below
- remaining_rows_2: float32 [16384, 1536], P(('leaf', 'front'))
- separator_rows_3: float32 [4096, 1536], P(('leaf', 'front')), as said below
- remaining_rows_3: float32 [8192, 1536], P(('leaf', 'front'))
- child_map_1: int32 [64, 8], replicated, may hold values from 0 to 11, as said below
- child_map_2: int32 [32, 8], replicated, may hold values from 0 to 11, as said below
- child_map_3: int32 [16, 8], replicated, may hold values from 0 to 11, as said below
Outputs:
- pivot_factor_1: float32 [16384, 512], P(('leaf', 'front'))
- below_factor_1: float32 [32768, 512], P(('leaf', 'front'))
- pivot_factor_2: float32 [8192, 512], P(('leaf', 'front'))
- below_factor_2: float32 [16384, 512], P(('leaf', 'front'))
- pivot_factor_3: float32 [4096, 512], P(('leaf', 'front'))
- below_factor_3: float32 [8192, 512], P(('leaf', 'front'))
Inputs may be any that keep to these rules, and one draw needn't show every extreme that they name: `child_map_1`: each row lists 8 distinct parent tiles in increasing order, the last one always 12 - 1. `child_map_2`: each row lists 8 distinct parent tiles in increasing order, the last one always 12 - 1. `child_map_3`: each row lists 8 distinct parent tiles in increasing order, the last one always 12 - 1. `leaf_update`: each block is symmetric positive definite, diagonal between 0.5 and 2, off-diagonal entries of magnitude about 0.008, smallest eigenvalue about 0.1 or more. Each front, separator_rows_1 above remaining_rows_1, is symmetric positive definite, diagonal between 2 and 4, off-diagonal entries of magnitude about 0.03, smallest eigenvalue about 0.35 or more. Each front, separator_rows_2 above remaining_rows_2, is symmetric positive definite, diagonal between 2 and 4, off-diagonal entries of magnitude about 0.03, smallest eigenvalue about 0.35 or more. Each front, separator_rows_3 above remaining_rows_3, is symmetric positive definite, diagonal between 2 and 4, off-diagonal entries of magnitude about 0.03, smallest eigenvalue about 0.35 or more.
All inputs are finite; a program needn't handle non-finite values.
Results may differ from a plain program's by a relative error of at most 0.0003.
Values sent between devices are 32-bit elements; how exact they have to be, the bound alone decides.
No kernel may reach another device: no remote copies, remote signals or barrier semaphores. Data moves between devices by JAX's collectives and lax.ppermute only.
A program may use at most 128 MiB of HBM per device.

v0:
```python
import jax
import jax.numpy as jnp
from jax import lax
from jax.sharding import PartitionSpec as P

TILE = 128
SEP = 512
UPD = 1024
NF = 1536
NT = 12
UT = 8


def from_partner(block, axis, stride):
    count = lax.axis_size(axis)
    route = []
    for low in range(count):
        high = low | 1 << stride
        if high != low and high < count:
            route += [(low, high), (high, low)]
    return lax.ppermute(block, axis, route)


def collect(pieces, depth_count):
    gathered = lax.all_gather(pieces, "front", axis=0, tiled=True)
    leaf_place = lax.axis_index("leaf")
    for bit_number in range(depth_count):
        partner = from_partner(gathered, "leaf", bit_number)
        on_high = leaf_place >> bit_number & 1 == 1
        gathered = jnp.where(
            on_high,
            jnp.concatenate([partner, gathered], axis=0),
            jnp.concatenate([gathered, partner], axis=0),
        )
    return gathered


def owned_rows(position, group_count):
    sep_count = SEP // group_count
    upd_count = UPD // group_count
    sep_index = position * sep_count + jnp.arange(sep_count, dtype=jnp.int32)
    upd_index = SEP + position * upd_count + jnp.arange(upd_count, dtype=jnp.int32)
    return jnp.concatenate([sep_index, upd_index])


def locate(tile_map, targets):
    tile_of = targets // TILE
    offset = targets % TILE
    matches = tile_map[None, :] == tile_of[:, None]
    present = jnp.any(matches, axis=1)
    slot_ids = jnp.arange(tile_map.shape[0], dtype=jnp.int32)
    source = jnp.sum(jnp.where(matches, slot_ids[None, :], 0), axis=1)
    return (source * TILE + offset, present)


def select_rows(full_update, tile_map, targets):
    source, present = locate(tile_map, targets)
    return jnp.where(present[:, None], jnp.take(full_update, source, axis=0), 0.0)


def expand_columns(row_block, tile_map):
    placing = (tile_map[:, None] == jnp.arange(NT, dtype=jnp.int32)[None, :]).astype(jnp.float32)
    tiled = row_block.reshape(row_block.shape[0], UT, TILE)
    placed = jnp.einsum("rut,un->rnt", tiled, placing, precision=lax.Precision.HIGHEST)
    return placed.reshape(row_block.shape[0], NF)


def body(
    leaf_update,
    separator_rows_1,
    remaining_rows_1,
    separator_rows_2,
    remaining_rows_2,
    separator_rows_3,
    remaining_rows_3,
    child_map_1,
    child_map_2,
    child_map_3,
):
    leaf_place = lax.axis_index("leaf")
    front_place = lax.axis_index("front")
    front_count = lax.axis_size("front")
    child_full = leaf_update
    sections = (
        (separator_rows_1, remaining_rows_1, child_map_1),
        (separator_rows_2, remaining_rows_2, child_map_2),
        (separator_rows_3, remaining_rows_3, child_map_3),
    )
    results = []
    for level_number in range(1, 4):
        sep_part, upd_part, child_maps = sections[level_number - 1]
        group_count = front_count * 2**level_number
        sep_count = SEP // group_count
        upd_count = UPD // group_count
        pair_bit = level_number - 1
        child_front = leaf_place >> pair_bit
        sibling_front = child_front ^ 1
        position = leaf_place % 2**level_number * front_count + front_place
        own_map = lax.dynamic_index_in_dim(child_maps, child_front, 0, keepdims=False)
        targets = owned_rows(position, group_count)
        sibling_map = lax.dynamic_index_in_dim(child_maps, sibling_front, 0, keepdims=False)
        sibling_full = from_partner(child_full, "leaf", pair_bit)
        sibling_block = select_rows(sibling_full, sibling_map, targets)
        own_term = expand_columns(select_rows(child_full, own_map, targets), own_map)
        sibling_term = expand_columns(sibling_block, sibling_map)
        is_odd = child_front & 1 == 1
        earlier_term = jnp.where(is_odd, sibling_term, own_term)
        later_term = jnp.where(is_odd, own_term, sibling_term)
        front_rows = jnp.concatenate([sep_part, upd_part], axis=0) + earlier_term + later_term
        panel_all = collect(front_rows[:, :SEP], level_number)
        blocks = panel_all.reshape(group_count, sep_count + upd_count, SEP)
        pivot_block = blocks[:, :sep_count].reshape(SEP, SEP)
        lower_block = blocks[:, sep_count:].reshape(UPD, SEP)
        diag_factor = jnp.linalg.cholesky(pivot_block)
        solved_all = lax.linalg.triangular_solve(
            diag_factor, lower_block, left_side=False, lower=True, transpose_a=True
        )
        solved_own = lax.dynamic_slice_in_dim(solved_all, position * upd_count, upd_count, 0)
        results.append(lax.dynamic_slice_in_dim(diag_factor, position * sep_count, sep_count, 0))
        results.append(solved_own)
        if level_number < 3:
            update_own = front_rows[sep_count:, SEP:] - jnp.dot(
                solved_own, solved_all.T, precision=lax.Precision.HIGHEST
            )
            child_full = collect(update_own, level_number)
    return (results[0], results[1], results[2], results[3], results[4], results[5])


def solution(mesh):
    in_specs = (
        P("leaf", None),
        P(("leaf", "front"), None),
        P(("leaf", "front"), None),
        P(("leaf", "front"), None),
        P(("leaf", "front"), None),
        P(("leaf", "front"), None),
        P(("leaf", "front"), None),
        P(),
        P(),
        P(),
    )
    out_specs = (
        P(("leaf", "front"), None),
        P(("leaf", "front"), None),
        P(("leaf", "front"), None),
        P(("leaf", "front"), None),
        P(("leaf", "front"), None),
        P(("leaf", "front"), None),
    )
    return jax.shard_map(body, mesh=mesh, in_specs=in_specs, out_specs=out_specs, check_vma=False)
```

profile of v0, /device:TPU:1, one launch (start us, length us, event | category | flops | bytes accessed | tf_op | source)
XLA Modules:
  0.0 1112.1 jit_solution(10254888534688105837)
XLA Ops:
  25.7 30.1 %all-gather.4.cloned.1.call-done = f32[768,512]{1,0:T(8,128)} async-done(((f32[192,512]{1,0:T(8,128)}), f32[768,512]{1,0:T(8,128)}) %all-gather.4.cloned.1.call-update) | async-done | bytes 1572880 | tf_op jit(solution)/shard_map/all_gather | solution.py:25
  66.7 11.7 %cholesky.374 = f32[128,128]{1,0:T(8,128)S(1)} custom-call(f32[128,128]{1,0:T(8,128)S(1)} %cholesky.586), custom_call_target="Cholesky" | custom-call | tf_op jit(solution)/shard_map/jit(cholesky)/cholesky | solution.py:114
  90.9 11.7 %cholesky.393 = f32[128,128]{1,0:T(8,128)S(1)} custom-call(f32[128,128]{1,0:T(8,128)S(1)} %cholesky.590), custom_call_target="Cholesky" | custom-call | tf_op jit(solution)/shard_map/jit(cholesky)/cholesky | solution.py:114
  102.7 10.0 custom-call.32
  114.2 11.7 %cholesky.414 = f32[128,128]{1,0:T(8,128)S(1)} custom-call(f32[128,128]{1,0:T(8,128)S(1)} %cholesky.595), custom_call_target="Cholesky" | custom-call | tf_op jit(solution)/shard_map/jit(cholesky)/cholesky | solution.py:114
  137.2 12.1 %cholesky.431 = f32[128,128]{1,0:T(8,128)S(1)} custom-call(f32[128,128]{1,0:T(8,128)S(1)} %convolution_subtract_fusion.10), custom_call_target="Cholesky" | custom-call | tf_op jit(solution)/shard_map/jit(cholesky)/cholesky | solution.py:114
  156.1 11.6 %while.6 = (s32[]{:T(128)}, f32[512,512]{1,0:T(8,128)}, s32[4,2]{0,1:T(2,128)S(1)}, f32[4,128,128]{2,1,0:T(8,128)S(1)}, s32[]{:T(128)}) while((s32[]{:T(128)}, f32[512,512]{1,0:T(8,128)}, s32[4,2]{0,1:T(2,128)S(1)}, f32[4,128,128]{2,1,0:T(8,128)S(1)}, s32[]{:T(128)}) %tuple.112), condition=%wide.while_cond, body=%wide.while_body.sunk | while | flops 2 | bytes 131189 | solution.py:115
  167.7 39.3 %custom-call.34 = f32[4,128,128]{1,2,0:T(8,128)S(1)} custom-call(f32[4,128,128]{2,1,0:T(8,128)S(1)} %get-tuple-element.31), custom_call_target="InvertDiagBlocksLowerTriangular" | custom-call | tf_op jit(solution)/shard_map/triangular_solve/custom-call.3 | solution.py:115
  222.2 33.3 %all-gather.6.cloned.1.call-done = f32[512,1024]{1,0:T(8,128)} async-done(((f32[128,1024]{1,0:T(8,128)}), f32[512,1024]{1,0:T(8,128)}) %all-gather.6.cloned.1.call-update) | async-done | bytes 2097168 | tf_op jit(solution)/shard_map/all_gather | solution.py:25
  270.9 86.6 %collective-permute-done.3 = f32[1024,1024]{1,0:T(8,128)} collective-permute-done((f32[1024,1024]{1,0:T(8,128)}, f32[1024,1024]{1,0:T(8,128)}, u32[]{:S(2)}, u32[]{:S(2)}) %collective-permute-start.3) | collective-permute-done | bytes 4194336 | tf_op jit(solution)/shard_map/ppermute | solution.py:21
  362.2 10.7 all_gather.17
  381.1 34.3 %collective-permute-done.5 = f32[768,512]{1,0:T(8,128)S(1)} collective-permute-done((f32[768,512]{1,0:T(8,128)S(1)}, f32[768,512]{1,0:T(8,128)S(1)}, u32[]{:S(2)}, u32[]{:S(2)}) %collective-permute-start.5) | collective-permute-done | bytes 1572896 | tf_op jit(solution)/shard_map/ppermute | solution.py:21
  419.8 11.7 %cholesky.446 = f32[128,128]{1,0:T(8,128)S(1)} custom-call(f32[128,128]{1,0:T(8,128)S(1)} %cholesky.599), custom_call_target="Cholesky" | custom-call | tf_op jit(solution)/shard_map/jit(cholesky)/cholesky | solution.py:114
  444.0 11.7 %cholesky.465 = f32[128,128]{1,0:T(8,128)S(1)} custom-call(f32[128,128]{1,0:T(8,128)S(1)} %cholesky.603), custom_call_target="Cholesky" | custom-call | tf_op jit(solution)/shard_map/jit(cholesky)/cholesky | solution.py:114
  455.7 10.2 custom-call.36
  467.5 11.7 %cholesky.486 = f32[128,128]{1,0:T(8,128)S(1)} custom-call(f32[128,128]{1,0:T(8,128)S(1)} %cholesky.608), custom_call_target="Cholesky" | custom-call | tf_op jit(solution)/shard_map/jit(cholesky)/cholesky | solution.py:114
  490.5 11.9 %cholesky.503 = f32[128,128]{1,0:T(8,128)S(1)} custom-call(f32[128,128]{1,0:T(8,128)S(1)} %convolution_subtract_fusion.9), custom_call_target="Cholesky" | custom-call | tf_op jit(solution)/shard_map/jit(cholesky)/cholesky | solution.py:114
  509.1 11.6 %while.7 = (s32[]{:T(128)}, f32[512,512]{1,0:T(8,128)}, s32[4,2]{0,1:T(2,128)S(1)}, f32[4,128,128]{2,1,0:T(8,128)S(1)}, s32[]{:T(128)}) while((s32[]{:T(128)}, f32[512,512]{1,0:T(8,128)}, s32[4,2]{0,1:T(2,128)S(1)}, f32[4,128,128]{2,1,0:T(8,128)S(1)}, s32[]{:T(128)}) %tuple.127), condition=%wide.while_cond.clone, body=%wide.while_body.clone.sunk | while | flops 2 | bytes 131189 | solution.py:115
  520.7 39.3 %custom-call.38 = f32[4,128,128]{1,2,0:T(8,128)S(1)} custom-call(f32[4,128,128]{2,1,0:T(8,128)S(1)} %get-tuple-element.32), custom_call_target="InvertDiagBlocksLowerTriangular" | custom-call | tf_op jit(solution)/shard_map/triangular_solve/custom-call.3 | solution.py:115
  574.4 26.1 %all-gather.8.cloned.1.call-done = f32[256,1024]{1,0:T(8,128)} async-done(((f32[64,1024]{1,0:T(8,128)}), f32[256,1024]{1,0:T(8,128)}) %all-gather.8.cloned.1.call-update) | async-done | bytes 1048592 | tf_op jit(solution)/shard_map/all_gather | solution.py:25
  608.2 45.6 %collective-permute-done.7 = f32[512,1024]{1,0:T(8,128)S(1)} collective-permute-done((f32[512,1024]{1,0:T(8,128)S(1)}, f32[512,1024]{1,0:T(8,128)S(1)}, u32[]{:S(2)}, u32[]{:S(2)}) %collective-permute-start.7) | collective-permute-done | bytes 2097184 | tf_op jit(solution)/shard_map/ppermute | solution.py:21
  662.4 176.2 %collective-permute-done.8 = f32[1024,1024]{1,0:T(8,128)} collective-permute-done((f32[1024,1024]{1,0:T(8,128)}, f32[1024,1024]{1,0:T(8,128)}, u32[]{:S(2)}, u32[]{:S(2)}) %collective-permute-start.8) | collective-permute-done | bytes 4194336 | tf_op jit(solution)/shard_map/ppermute | solution.py:21
  842.6 10.9 all_gather.19
  858.5 18.7 %collective-permute-done.10 = f32[384,512]{1,0:T(8,128)S(1)} collective-permute-done((f32[384,512]{1,0:T(8,128)S(1)}, f32[384,512]{1,0:T(8,128)S(1)}, u32[]{:S(2)}, u32[]{:S(2)}) %collective-permute-start.10) | collective-permute-done | bytes 786464 | tf_op jit(solution)/shard_map/ppermute | solution.py:21
  885.1 62.8 %collective-permute-done.11 = f32[768,512]{1,0:T(8,128)S(1)} collective-permute-done((f32[768,512]{1,0:T(8,128)S(1)}, f32[768,512]{1,0:T(8,128)S(1)}, u32[]{:S(2)}, u32[]{:S(2)}) %collective-permute-start.11) | collective-permute-done | bytes 1572896 | tf_op jit(solution)/shard_map/ppermute | solution.py:21
  952.3 11.7 %cholesky.518 = f32[128,128]{1,0:T(8,128)S(1)} custom-call(f32[128,128]{1,0:T(8,128)S(1)} %cholesky.612), custom_call_target="Cholesky" | custom-call | tf_op jit(solution)/shard_map/jit(cholesky)/cholesky | solution.py:114
  976.5 11.7 %cholesky.537 = f32[128,128]{1,0:T(8,128)S(1)} custom-call(f32[128,128]{1,0:T(8,128)S(1)} %cholesky.616), custom_call_target="Cholesky" | custom-call | tf_op jit(solution)/shard_map/jit(cholesky)/cholesky | solution.py:114
  988.2 9.9 custom-call.40
  999.8 11.7 %cholesky.558 = f32[128,128]{1,0:T(8,128)S(1)} custom-call(f32[128,128]{1,0:T(8,128)S(1)} %cholesky.621), custom_call_target="Cholesky" | custom-call | tf_op jit(solution)/shard_map/jit(cholesky)/cholesky | solution.py:114
  1022.8 11.9 %cholesky.575 = f32[128,128]{1,0:T(8,128)S(1)} custom-call(f32[128,128]{1,0:T(8,128)S(1)} %convolution_subtract_fusion.8), custom_call_target="Cholesky" | custom-call | tf_op jit(solution)/shard_map/jit(cholesky)/cholesky | solution.py:114
  1041.6 11.5 %while.8 = (s32[]{:T(128)}, f32[512,512]{1,0:T(8,128)}, s32[4,2]{0,1:T(2,128)S(1)}, f32[4,128,128]{2,1,0:T(8,128)S(1)}, s32[]{:T(128)}) while((s32[]{:T(128)}, f32[512,512]{1,0:T(8,128)}, s32[4,2]{0,1:T(2,128)S(1)}, f32[4,128,128]{2,1,0:T(8,128)S(1)}, s32[]{:T(128)}) %tuple.128), condition=%wide.while_cond.clone.1, body=%wide.while_body.clone.1.sunk | while | flops 2 | bytes 131189 | solution.py:115
  1053.0 39.3 %custom-call.42 = f32[4,128,128]{1,2,0:T(8,128)S(1)} custom-call(f32[4,128,128]{2,1,0:T(8,128)S(1)} %get-tuple-element.33), custom_call_target="InvertDiagBlocksLowerTriangular" | custom-call | tf_op jit(solution)/shard_map/triangular_solve/custom-call.3 | solution.py:115
  (266 shorter events, 264.4 us)
Async XLA Ops:
  7.2 48.7 %all-gather.4.cloned.1.call-start = ((), (), s32[]{:S(2)}) async-start(), calls=%async_computation | async-start | bytes 1966080 | tf_op jit(solution)/shard_map/all_gather | solution.py:25
  7.2 10.5 collective-permute-start
  21.5 1.1 copy-start.6
  21.5 1.2 copy-start.8
  23.9 1.0 copy-start.3
  25.7 229.8 %all-gather.6.cloned.1.call-start = ((), (), s32[]{:S(2)}) async-start(), calls=%async_computation.1 | async-start | bytes 2621440 | tf_op jit(solution)/shard_map/all_gather | solution.py:25
  55.9 4.4 collective-permute-start.1
  65.7 1.0 copy-start
  218.2 0.7 copy-start.4
  222.1 378.4 %all-gather.8.cloned.1.call-start = ((), (), s32[]{:S(2)}) async-start(), calls=%async_computation.2 | async-start | bytes 1310720 | tf_op jit(solution)/shard_map/all_gather | solution.py:25
  255.5 4.8 collective-permute-start.2
  265.4 92.1 %collective-permute-start.3 = (f32[1024,1024]{1,0:T(8,128)}, f32[1024,1024]{1,0:T(8,128)}, u32[]{:S(2)}, u32[]{:S(2)}) collective-permute-start(f32[1024,1024]{1,0:T(8,128)} %maximum_select_fusion), channel_id=1, source_target_pairs={{0,8},{8,0},{4,12},{12,4},{16,24},{24,16},{20,28},{28,20},{32,40},... | collective-permute-start | bytes 12582920 | tf_op jit(solution)/shard_map/ppermute | solution.py:21
  360.6 1.0 copy-start.7
  360.6 1.0 copy-start.10
  362.2 15.5 %copy-start.5 = (f32[96,1536]{1,0:T(8,128)}, f32[96,1536]{1,0:T(8,128)S(1)}, u32[]{:S(2)}) copy-start(f32[96,1536]{1,0:T(8,128)S(1)} %bitcast_add_fusion.5) | copy-start | bytes 1769476
  372.9 6.7 collective-permute-start.4
  379.7 35.7 %collective-permute-start.5 = (f32[768,512]{1,0:T(8,128)S(1)}, f32[768,512]{1,0:T(8,128)S(1)}, u32[]{:S(2)}, u32[]{:S(2)}) collective-permute-start(f32[768,512]{1,0:T(8,128)S(1)} %maximum_select_fusion.6), channel_id=1, source_target_pairs={{0,8},{8,0},{4,12},{12,4},{16,24},{24,16},{20,28},{28,20},{32,40},... | collective-permute-start | bytes 4718600 | tf_op jit(solution)/shard_map/ppermute | solution.py:21
  418.8 1.0 copy-start.1
  600.5 4.5 collective-permute-start.6
  606.8 51.6 %copy-start.12 = (s32[16,8]{0,1:T(8,128)S(1)}, s32[16,8]{0,1:T(8,128)}, u32[]{:S(2)}) copy-start(s32[16,8]{0,1:T(8,128)} %param.28) | copy-start | bytes 1540
  606.8 46.9 %collective-permute-start.7 = (f32[512,1024]{1,0:T(8,128)S(1)}, f32[512,1024]{1,0:T(8,128)S(1)}, u32[]{:S(2)}, u32[]{:S(2)}) collective-permute-start(f32[512,1024]{1,0:T(8,128)S(1)} %maximum_select_fusion.5), channel_id=1, source_target_pairs={{0,8},{8,0},{4,12},{12,4},{16,24},{24,16},{20,28},{28,20},{32,40},... | collective-permute-start | bytes 6291464 | tf_op jit(solution)/shard_map/ppermute | solution.py:21
  656.1 182.5 %collective-permute-start.8 = (f32[1024,1024]{1,0:T(8,128)}, f32[1024,1024]{1,0:T(8,128)}, u32[]{:S(2)}, u32[]{:S(2)}) collective-permute-start(f32[1024,1024]{1,0:T(8,128)} %maximum_select_fusion.1), channel_id=1, source_target_pairs={{0,16},{16,0},{4,20},{20,4},{8,24},{24,8},{12,28},{28,12},{32,48},... | collective-permute-start | bytes 12582920 | tf_op jit(solution)/shard_map/ppermute | solution.py:21
  841.6 0.9 copy-start.9
  841.6 1.0 copy-start.11
  853.5 4.9 collective-permute-start.9
  858.4 18.8 %collective-permute-start.10 = (f32[384,512]{1,0:T(8,128)S(1)}, f32[384,512]{1,0:T(8,128)S(1)}, u32[]{:S(2)}, u32[]{:S(2)}) collective-permute-start(f32[384,512]{1,0:T(8,128)S(1)} %maximum_select_fusion.8), channel_id=1, source_target_pairs={{0,8},{8,0},{4,12},{12,4},{16,24},{24,16},{20,28},{28,20},{32,40},... | collective-permute-start | bytes 2359304 | tf_op jit(solution)/shard_map/ppermute | solution.py:21
  877.5 70.5 %collective-permute-start.11 = (f32[768,512]{1,0:T(8,128)S(1)}, f32[768,512]{1,0:T(8,128)S(1)}, u32[]{:S(2)}, u32[]{:S(2)}) collective-permute-start(f32[768,512]{1,0:T(8,128)S(1)} %maximum_select_fusion.7), channel_id=1, source_target_pairs={{0,16},{16,0},{4,20},{20,4},{8,24},{24,8},{12,28},{28,12},{32,48},... | collective-permute-start | bytes 4718600 | tf_op jit(solution)/shard_map/ppermute | solution.py:21
  951.3 1.0 copy-start.2
Sparse Core Ops, SparseCore 0:
  25.8 30.0 all-gather.3
  222.2 33.1 all-gather.5
  574.6 25.8 all-gather.7
where the time goes:
time: 1120 us; the launch traced here: 1110 us
  waiting for transfers between devices  528 us (47%)
  other arithmetic  382 us (34%)
  local copies, waits for them, and re-layouts  74.5 us (7%)
  matrix products  59 us (5%)
  starting transfers between devices  24.1 us (2%)
  between operations  22.8 us (2%)
  blocking collectives  21.5 us (2%)
    ppermute x12, waiting for transfers between devices, from_partner(): return lax.ppermute(block, axis, route)  438 us
    another operation x45, other arithmetic, body(): diag_factor = jnp.linalg.cholesky(pivot_block)  238 us
    another operation x10, other arithmetic, body(): lax.linalg.triangular_solve(diag_factor, lower_block, left_side=False, lo...  123 us
    all_gather x3, waiting for transfers between devices, collect(): gathered = lax.all_gather(pieces, 'front', axis=0, tiled=True)  89.5 us
    another operation x40, local copies, waits for them, and re-layouts, body(): lax.linalg.triangular_solve(diag_factor, lower_block, left_side=False, lo...  34.4 us
    another operation x21, matrix products, body(): lax.linalg.triangular_solve(diag_factor, lower_block, left_side=False, lo...  32.4 us
    ppermute x12, starting transfers between devices, from_partner(): return lax.ppermute(block, axis, route)  24 us
  transfers between devices with their start and end apart: 15, of which 15 were waited for; matrix products, arithmetic and copies ran while one was open for 2% of the time, Pallas kernels for 0%

commit v1 on v0

--- a/solution.py
+++ b/solution.py
@@ -22,7 +22,9 @@
 
 
 def collect(pieces, depth_count):
-    gathered = lax.all_gather(pieces, "front", axis=0, tiled=True)
+    gathered = jnp.concatenate(
+        lax.all_to_all(jnp.stack([pieces] * lax.axis_size("front")), "front", 0, 0), axis=0
+    )
     leaf_place = lax.axis_index("leaf")
     for bit_number in range(depth_count):
         partner = from_partner(gathered, "leaf", bit_number)

time: 1120 us -> 1080 us (0.964)
  waiting for transfers between devices: 528 us -> 435 us
  blocking collectives: 21.5 us -> 89.9 us
  between operations: 22.8 us -> 9.94 us
    all_to_all x0 -> x5, blocking collectives: none -> 89.9 us  [collect(): lax.all_to_all(jnp.stack([pieces] * lax.axis_size('front')), 'front', 0, 0)]
    all_gather x3 -> x0, waiting for transfers between devices: 89.5 us -> none  [collect(): gathered = lax.all_gather(pieces, 'front', axis=0, tiled=True)]
    all_gather x2 -> x0, blocking collectives: 21.5 us -> none  [collect(): gathered = lax.all_gather(pieces, 'front', axis=0, tiled=True)]
  transfers between devices with their start and end apart: 15 -> 12, of which waited for: 15 -> 12; matrix products, arithmetic and copies ran while one was open for 2% -> 2% of each run, Pallas kernels for 0% -> 0%
where the time goes in v1:
time: 1080 us; the launch traced here: 1070 us
  waiting for transfers between devices  435 us (40%)
  other arithmetic  375 us (35%)
  blocking collectives  89.9 us (8%)
  local copies, waits for them, and re-layouts  72.8 us (7%)
  matrix products  57.6 us (5%)
  starting transfers between devices  26.9 us (2%)
    ppermute x12, waiting for transfers between devices, from_partner(): return lax.ppermute(block, axis, route)  435 us
    another operation x45, other arithmetic, body(): diag_factor = jnp.linalg.cholesky(pivot_block)  238 us
    another operation x10, other arithmetic, body(): lax.linalg.triangular_solve(diag_factor, lower_block, left_side=False, lo...  123 us
    all_to_all x5, blocking collectives, collect(): lax.all_to_all(jnp.stack([pieces] * lax.axis_size('front')), 'front', 0, 0)  89.9 us
    another operation x40, local copies, waits for them, and re-layouts, body(): lax.linalg.triangular_solve(diag_factor, lower_block, left_side=False, lo...  34.4 us
    another operation x21, matrix products, body(): lax.linalg.triangular_solve(diag_factor, lower_block, left_side=False, lo...  32.4 us
    ppermute x12, starting transfers between devices, from_partner(): return lax.ppermute(block, axis, route)  26.9 us
  transfers between devices with their start and end apart: 12, of which 12 were waited for; matrix products, arithmetic and copies ran while one was open for 2% of the time, Pallas kernels for 0%

profile of v1, /device:TPU:1, one launch (start us, length us, event | category | flops | bytes accessed | tf_op | source)
XLA Modules:
  0.0 1068.0 jit_solution(13864724606370952503)
XLA Ops:
  17.5 22.8 %all_to_all.25 = f32[4,192,512]{2,1,0:T(8,128)S(1)} all-to-all(f32[4,192,512]{2,1,0:T(8,128)S(1)} %stack.10), channel_id=1, replica_groups=mesh['leaf'=64,'front'=4] {'front'}, dimensions={0} | all-to-all | bytes 3145728 | tf_op jit(solution)/shard_map/all_to_all | solution.py:26
  49.3 11.7 %cholesky.374 = f32[128,128]{1,0:T(8,128)S(1)} custom-call(f32[128,128]{1,0:T(8,128)S(1)} %cholesky.586), custom_call_target="Cholesky" | custom-call | tf_op jit(solution)/shard_map/jit(cholesky)/cholesky | solution.py:116
  73.5 11.7 %cholesky.393 = f32[128,128]{1,0:T(8,128)S(1)} custom-call(f32[128,128]{1,0:T(8,128)S(1)} %cholesky.590), custom_call_target="Cholesky" | custom-call | tf_op jit(solution)/shard_map/jit(cholesky)/cholesky | solution.py:116
  85.3 10.2 custom-call.32
  97.1 11.7 %cholesky.414 = f32[128,128]{1,0:T(8,128)S(1)} custom-call(f32[128,128]{1,0:T(8,128)S(1)} %cholesky.595), custom_call_target="Cholesky" | custom-call | tf_op jit(solution)/shard_map/jit(cholesky)/cholesky | solution.py:116
  108.8 9.8 custom-call.33
  120.1 11.7 %cholesky.431 = f32[128,128]{1,0:T(8,128)S(1)} custom-call(f32[128,128]{1,0:T(8,128)S(1)} %convolution_subtract_fusion.10), custom_call_target="Cholesky" | custom-call | tf_op jit(solution)/shard_map/jit(cholesky)/cholesky | solution.py:116
  138.7 11.7 %while.6 = (s32[]{:T(128)}, f32[512,512]{1,0:T(8,128)}, s32[4,2]{0,1:T(2,128)S(1)}, f32[4,128,128]{2,1,0:T(8,128)S(1)}, s32[]{:T(128)}) while((s32[]{:T(128)}, f32[512,512]{1,0:T(8,128)}, s32[4,2]{0,1:T(2,128)S(1)}, f32[4,128,128]{2,1,0:T(8,128)S(1)}, s32[]{:T(128)}) %tuple.112), condition=%wide.while_cond, body=%wide.while_body.sunk | while | flops 2 | bytes 131189 | solution.py:117
  150.4 39.3 %custom-call.34 = f32[4,128,128]{1,2,0:T(8,128)S(1)} custom-call(f32[4,128,128]{2,1,0:T(8,128)S(1)} %get-tuple-element.31), custom_call_target="InvertDiagBlocksLowerTriangular" | custom-call | tf_op jit(solution)/shard_map/triangular_solve/custom-call.3 | solution.py:117
  203.7 28.6 %all_to_all.26 = f32[4,128,1024]{2,1,0:T(8,128)S(1)} all-to-all(f32[4,128,1024]{2,1,0:T(8,128)S(1)} %stack.11), channel_id=1, replica_groups=mesh['leaf'=64,'front'=4] {'front'}, dimensions={0} | all-to-all | bytes 4194304 | tf_op jit(solution)/shard_map/all_to_all | solution.py:26
  245.5 86.4 %collective-permute-done.3 = f32[1024,1024]{1,0:T(8,128)} collective-permute-done((f32[1024,1024]{1,0:T(8,128)}, f32[1024,1024]{1,0:T(8,128)}, u32[]{:S(2)}, u32[]{:S(2)}) %collective-permute-start.3) | collective-permute-done | bytes 4194336 | tf_op jit(solution)/shard_map/ppermute | solution.py:21
  336.7 13.5 %all_to_all.27 = f32[4,96,512]{2,1,0:T(8,128)S(1)} all-to-all(f32[4,96,512]{2,1,0:T(8,128)S(1)} %stack.12), channel_id=1, replica_groups=mesh['leaf'=64,'front'=4] {'front'}, dimensions={0} | all-to-all | bytes 1572864 | tf_op jit(solution)/shard_map/all_to_all | solution.py:26
  356.4 34.2 %collective-permute-done.5 = f32[768,512]{1,0:T(8,128)S(1)} collective-permute-done((f32[768,512]{1,0:T(8,128)S(1)}, f32[768,512]{1,0:T(8,128)S(1)}, u32[]{:S(2)}, u32[]{:S(2)}) %collective-permute-start.5) | collective-permute-done | bytes 1572896 | tf_op jit(solution)/shard_map/ppermute | solution.py:21
  394.8 11.7 %cholesky.446 = f32[128,128]{1,0:T(8,128)S(1)} custom-call(f32[128,128]{1,0:T(8,128)S(1)} %cholesky.599), custom_call_target="Cholesky" | custom-call | tf_op jit(solution)/shard_map/jit(cholesky)/cholesky | solution.py:116
  419.1 11.7 %cholesky.465 = f32[128,128]{1,0:T(8,128)S(1)} custom-call(f32[128,128]{1,0:T(8,128)S(1)} %cholesky.603), custom_call_target="Cholesky" | custom-call | tf_op jit(solution)/shard_map/jit(cholesky)/cholesky | solution.py:116
  430.8 10.0 custom-call.36
  442.3 11.7 %cholesky.486 = f32[128,128]{1,0:T(8,128)S(1)} custom-call(f32[128,128]{1,0:T(8,128)S(1)} %cholesky.608), custom_call_target="Cholesky" | custom-call | tf_op jit(solution)/shard_map/jit(cholesky)/cholesky | solution.py:116
  465.4 11.7 %cholesky.503 = f32[128,128]{1,0:T(8,128)S(1)} custom-call(f32[128,128]{1,0:T(8,128)S(1)} %convolution_subtract_fusion.9), custom_call_target="Cholesky" | custom-call | tf_op jit(solution)/shard_map/jit(cholesky)/cholesky | solution.py:116
  483.8 11.8 %while.7 = (s32[]{:T(128)}, f32[512,512]{1,0:T(8,128)}, s32[4,2]{0,1:T(2,128)S(1)}, f32[4,128,128]{2,1,0:T(8,128)S(1)}, s32[]{:T(128)}) while((s32[]{:T(128)}, f32[512,512]{1,0:T(8,128)}, s32[4,2]{0,1:T(2,128)S(1)}, f32[4,128,128]{2,1,0:T(8,128)S(1)}, s32[]{:T(128)}) %tuple.121), condition=%wide.while_cond.clone, body=%wide.while_body.clone.sunk | while | flops 2 | bytes 131189 | solution.py:117
  495.6 39.3 %custom-call.38 = f32[4,128,128]{1,2,0:T(8,128)S(1)} custom-call(f32[4,128,128]{2,1,0:T(8,128)S(1)} %get-tuple-element.32), custom_call_target="InvertDiagBlocksLowerTriangular" | custom-call | tf_op jit(solution)/shard_map/triangular_solve/custom-call.3 | solution.py:117
  548.7 16.4 %all_to_all.28 = f32[4,64,1024]{2,1,0:T(8,128)S(1)} all-to-all(f32[4,64,1024]{2,1,0:T(8,128)S(1)} %stack.13), channel_id=1, replica_groups=mesh['leaf'=64,'front'=4] {'front'}, dimensions={0} | all-to-all | bytes 2097152 | tf_op jit(solution)/shard_map/all_to_all | solution.py:26
  571.7 45.4 %collective-permute-done.7 = f32[512,1024]{1,0:T(8,128)S(1)} collective-permute-done((f32[512,1024]{1,0:T(8,128)S(1)}, f32[512,1024]{1,0:T(8,128)S(1)}, u32[]{:S(2)}, u32[]{:S(2)}) %collective-permute-start.7) | collective-permute-done | bytes 2097184 | tf_op jit(solution)/shard_map/ppermute | solution.py:21
  626.6 176.1 %collective-permute-done.8 = f32[1024,1024]{1,0:T(8,128)} collective-permute-done((f32[1024,1024]{1,0:T(8,128)}, f32[1024,1024]{1,0:T(8,128)}, u32[]{:S(2)}, u32[]{:S(2)}) %collective-permute-start.8) | collective-permute-done | bytes 4194336 | tf_op jit(solution)/shard_map/ppermute | solution.py:21
  821.2 17.3 %collective-permute-done.10 = f32[384,512]{1,0:T(8,128)S(1)} collective-permute-done((f32[384,512]{1,0:T(8,128)S(1)}, f32[384,512]{1,0:T(8,128)S(1)}, u32[]{:S(2)}, u32[]{:S(2)}) %collective-permute-start.10) | collective-permute-done | bytes 786464 | tf_op jit(solution)/shard_map/ppermute | solution.py:21
  847.9 62.1 %collective-permute-done.11 = f32[768,512]{1,0:T(8,128)S(1)} collective-permute-done((f32[768,512]{1,0:T(8,128)S(1)}, f32[768,512]{1,0:T(8,128)S(1)}, u32[]{:S(2)}, u32[]{:S(2)}) %collective-permute-start.11) | collective-permute-done | bytes 1572896 | tf_op jit(solution)/shard_map/ppermute | solution.py:21
  914.4 11.7 %cholesky.518 = f32[128,128]{1,0:T(8,128)S(1)} custom-call(f32[128,128]{1,0:T(8,128)S(1)} %cholesky.612), custom_call_target="Cholesky" | custom-call | tf_op jit(solution)/shard_map/jit(cholesky)/cholesky | solution.py:116
  938.6 11.7 %cholesky.537 = f32[128,128]{1,0:T(8,128)S(1)} custom-call(f32[128,128]{1,0:T(8,128)S(1)} %cholesky.616), custom_call_target="Cholesky" | custom-call | tf_op jit(solution)/shard_map/jit(cholesky)/cholesky | solution.py:116
  950.3 10.0 custom-call.40
  961.9 11.7 %cholesky.558 = f32[128,128]{1,0:T(8,128)S(1)} custom-call(f32[128,128]{1,0:T(8,128)S(1)} %cholesky.621), custom_call_target="Cholesky" | custom-call | tf_op jit(solution)/shard_map/jit(cholesky)/cholesky | solution.py:116
  984.9 12.0 %cholesky.575 = f32[128,128]{1,0:T(8,128)S(1)} custom-call(f32[128,128]{1,0:T(8,128)S(1)} %convolution_subtract_fusion.8), custom_call_target="Cholesky" | custom-call | tf_op jit(solution)/shard_map/jit(cholesky)/cholesky | solution.py:116
  1003.7 11.5 %while.8 = (s32[]{:T(128)}, f32[512,512]{1,0:T(8,128)}, s32[4,2]{0,1:T(2,128)S(1)}, f32[4,128,128]{2,1,0:T(8,128)S(1)}, s32[]{:T(128)}) while((s32[]{:T(128)}, f32[512,512]{1,0:T(8,128)}, s32[4,2]{0,1:T(2,128)S(1)}, f32[4,128,128]{2,1,0:T(8,128)S(1)}, s32[]{:T(128)}) %tuple.122), condition=%wide.while_cond.clone.1, body=%wide.while_body.clone.1.sunk | while | flops 2 | bytes 131189 | solution.py:117
  1015.2 39.3 %custom-call.42 = f32[4,128,128]{1,2,0:T(8,128)S(1)} custom-call(f32[4,128,128]{2,1,0:T(8,128)S(1)} %get-tuple-element.33), custom_call_target="InvertDiagBlocksLowerTriangular" | custom-call | tf_op jit(solution)/shard_map/triangular_solve/custom-call.3 | solution.py:117
  (265 shorter events, 255.9 us)
Async XLA Ops:
  0.6 10.5 collective-permute-start
  14.9 1.1 copy-start.6
  14.9 1.2 copy-start.8
  17.3 23.1 %copy-start.3 = (f32[192,1536]{1,0:T(8,128)}, f32[192,1536]{1,0:T(8,128)S(1)}, u32[]{:S(2)}) copy-start(f32[192,1536]{1,0:T(8,128)S(1)} %bitcast_add_fusion) | copy-start | bytes 3538948
  40.4 4.5 collective-permute-start.1
  48.3 1.0 copy-start
  200.9 2.7 copy-start.4
  232.3 5.2 collective-permute-start.2
  239.8 92.1 %collective-permute-start.3 = (f32[1024,1024]{1,0:T(8,128)}, f32[1024,1024]{1,0:T(8,128)}, u32[]{:S(2)}, u32[]{:S(2)}) collective-permute-start(f32[1024,1024]{1,0:T(8,128)} %maximum_select_fusion), channel_id=1, source_target_pairs={{0,8},{8,0},{4,12},{12,4},{16,24},{24,16},{20,28},{28,20},{32,40},... | collective-permute-start | bytes 12582920 | tf_op jit(solution)/shard_map/ppermute | solution.py:21
  335.0 1.0 copy-start.7
  335.0 1.0 copy-start.10
  336.6 15.8 %copy-start.5 = (f32[96,1536]{1,0:T(8,128)}, f32[96,1536]{1,0:T(8,128)S(1)}, u32[]{:S(2)}) copy-start(f32[96,1536]{1,0:T(8,128)S(1)} %bitcast_add_fusion.5) | copy-start | bytes 1769476
  350.2 4.0 collective-permute-start.4
  354.4 36.1 %collective-permute-start.5 = (f32[768,512]{1,0:T(8,128)S(1)}, f32[768,512]{1,0:T(8,128)S(1)}, u32[]{:S(2)}, u32[]{:S(2)}) collective-permute-start(f32[768,512]{1,0:T(8,128)S(1)} %maximum_select_fusion.6), channel_id=1, source_target_pairs={{0,8},{8,0},{4,12},{12,4},{16,24},{24,16},{20,28},{28,20},{32,40},... | collective-permute-start | bytes 4718600 | tf_op jit(solution)/shard_map/ppermute | solution.py:21
  393.8 1.0 copy-start.1
  565.1 4.8 collective-permute-start.6
  570.1 52.5 %copy-start.12 = (s32[16,8]{0,1:T(8,128)S(1)}, s32[16,8]{0,1:T(8,128)}, u32[]{:S(2)}) copy-start(s32[16,8]{0,1:T(8,128)} %param.28) | copy-start | bytes 1540
  570.1 46.9 %collective-permute-start.7 = (f32[512,1024]{1,0:T(8,128)S(1)}, f32[512,1024]{1,0:T(8,128)S(1)}, u32[]{:S(2)}, u32[]{:S(2)}) collective-permute-start(f32[512,1024]{1,0:T(8,128)S(1)} %maximum_select_fusion.5), channel_id=1, source_target_pairs={{0,8},{8,0},{4,12},{12,4},{16,24},{24,16},{20,28},{28,20},{32,40},... | collective-permute-start | bytes 6291464 | tf_op jit(solution)/shard_map/ppermute | solution.py:21
  619.4 183.4 %collective-permute-start.8 = (f32[1024,1024]{1,0:T(8,128)}, f32[1024,1024]{1,0:T(8,128)}, u32[]{:S(2)}, u32[]{:S(2)}) collective-permute-start(f32[1024,1024]{1,0:T(8,128)} %maximum_select_fusion.1), channel_id=1, source_target_pairs={{0,16},{16,0},{4,20},{20,4},{8,24},{24,8},{12,28},{28,12},{32,48},... | collective-permute-start | bytes 12582920 | tf_op jit(solution)/shard_map/ppermute | solution.py:21
  805.7 0.9 copy-start.9
  805.7 1.0 copy-start.11
  815.5 4.1 collective-permute-start.9
  819.6 18.9 %collective-permute-start.10 = (f32[384,512]{1,0:T(8,128)S(1)}, f32[384,512]{1,0:T(8,128)S(1)}, u32[]{:S(2)}, u32[]{:S(2)}) collective-permute-start(f32[384,512]{1,0:T(8,128)S(1)} %maximum_select_fusion.8), channel_id=1, source_target_pairs={{0,8},{8,0},{4,12},{12,4},{16,24},{24,16},{20,28},{28,20},{32,40},... | collective-permute-start | bytes 2359304 | tf_op jit(solution)/shard_map/ppermute | solution.py:21
  838.7 71.4 %collective-permute-start.11 = (f32[768,512]{1,0:T(8,128)S(1)}, f32[768,512]{1,0:T(8,128)S(1)}, u32[]{:S(2)}, u32[]{:S(2)}) collective-permute-start(f32[768,512]{1,0:T(8,128)S(1)} %maximum_select_fusion.7), channel_id=1, source_target_pairs={{0,16},{16,0},{4,20},{20,4},{8,24},{24,8},{12,28},{28,12},{32,48},... | collective-permute-start | bytes 4718600 | tf_op jit(solution)/shard_map/ppermute | solution.py:21
  913.4 1.0 copy-start.2
